TPU v7x, 32 devices: a whole 2x2x4 slice. The times are simulated.
32 devices in a mesh: groups: 2 (over x), port: 16 (over z, y, core).
Axes of the slice: x: 2, y: 2, z: 4, core: 2. Of those that a mesh axis runs over, the one named last changes fastest.
Arguments:
- measured: bfloat16 [4, 2, 4096, 4096], P('groups', None, 'port'), parts along dimension 0, may hold values from -6 to 6
- out_factor: bfloat16 [4096, 1024], P('port', 'groups'), parts along dimension 1, may hold values from -0.25 to 0.25
- in_factor: bfloat16 [1024, 4096], P('groups', 'port'), parts along dimension 0, may hold values from -6 to 6
- pole_rates: float32 [1024], P('groups'), parts along dimension 0, may hold values from 0.1 to 10
- freq_index: int32 [4], P('groups'), parts along dimension 0, may hold values from 0 to 1023
- quad_codes: int32 [4], P('groups'), parts along dimension 0, may hold values from 1 to 4
Outputs:
- grad_out: float32 [4096, 1024], P('port', 'groups'), parts along dimension 1
- grad_in_t: float32 [4096, 1024], P('port', 'groups'), parts along dimension 1
There are 2 independent parts, one for each index of `groups`. A program takes and returns all parts, laid end to end along the dimension named above; each array names one. Nothing has to cross between parts.
All inputs are finite; a program needn't handle non-finite values.
Results may differ from a plain program's by a relative error of at most 0.002.
Values may be sent and summed in bfloat16 or wider, within the bound.
A program may use at most 64 MiB of HBM per device.

v0:
```python
import math
import jax
import jax.numpy as jnp
from jax import lax
from jax.sharding import PartitionSpec as P

GRID = 1024
low_freq = 0.1
log_span = math.log(100.0)


def pole_terms(freq_index, pole_rates):
    omega = low_freq * jnp.exp(log_span * freq_index.astype(jnp.float32) / (GRID - 1))
    denominator = pole_rates[None, :] * pole_rates[None, :] + omega[:, None] * omega[:, None]
    real_side = pole_rates[None, :] / denominator
    imag_side = -omega[:, None] / denominator
    return jnp.stack([real_side, imag_side], axis=1)


def contract_first(left, right):
    return lax.dot_general(
        left, right, (((0,), (0,)), ((), ())), preferred_element_type=jnp.float32
    )


def contract_second(left, right):
    return lax.dot_general(
        left, right, (((1,), (1,)), ((), ())), preferred_element_type=jnp.float32
    )


def on_device(measured, out_factor, in_factor, pole_rates, freq_index, quad_codes):
    freq_count = measured.shape[0]
    local_rows = out_factor.shape[0]
    pole_count = out_factor.shape[1]
    local_cols = in_factor.shape[1]
    total_in = measured.shape[3]
    total_out = local_rows * lax.axis_size("port")
    coefficients = pole_terms(freq_index, pole_rates)
    weights = quad_codes.astype(jnp.float32) * 0.25
    weighted = weights[:, None, None] * coefficients
    scaled = (
        out_factor.astype(jnp.float32)[None, None, :, :] * coefficients[:, :, None, :]
    ).astype(jnp.bfloat16)
    block_cols = lax.all_gather(in_factor, "port", axis=1, tiled=True)
    width_cols = block_cols.shape[1]
    model = jnp.dot(scaled.reshape(-1, pole_count), block_cols, preferred_element_type=jnp.float32)
    model = model.reshape(freq_count, 2, local_rows, width_cols)
    residual = (model - measured.astype(jnp.float32)).astype(jnp.bfloat16)
    update = contract_second(residual.reshape(-1, width_cols), block_cols)
    update = update.reshape(freq_count, 2, local_rows, pole_count)
    grad_out = jnp.zeros((local_rows, pole_count), jnp.float32)
    for freq_slot in range(freq_count):
        for comp_slot in range(2):
            grad_out = (
                grad_out + weighted[freq_slot, comp_slot][None, :] * update[freq_slot, comp_slot]
            )
    grad_out = grad_out * (1.0 / math.sqrt(total_in))
    running = jnp.zeros((local_cols * lax.axis_size("port"), pole_count), jnp.float32)
    for freq_slot in range(freq_count):
        for comp_slot in range(2):
            running = running + weighted[freq_slot, comp_slot][None, :] * contract_first(
                residual[freq_slot, comp_slot], out_factor
            )
    grad_in_t = lax.psum_scatter(running, "port", scatter_dimension=0, tiled=True)
    grad_in_t = grad_in_t * (1.0 / math.sqrt(total_out))
    return (grad_out, grad_in_t)


def solution(mesh):
    in_specs = (
        P("groups", None, "port", None),
        P("port", "groups"),
        P("groups", "port"),
        P("groups"),
        P("groups"),
        P("groups"),
    )
    out_specs = (P("port", "groups"), P("port", "groups"))
    return jax.shard_map(
        on_device, mesh=mesh, in_specs=in_specs, out_specs=out_specs, check_vma=False
    )
```

profile of v0, /device:TPU:0, one launch (start us, length us, event | category | flops | bytes accessed | tf_op | source)
XLA Modules:
  0.0 206.1 jit_solution(8669891354242152455)
XLA Ops:
  7.2 0.0 all-gather.2.cloned.1.call-start
  7.2 0.7 all-gather.2.cloned.1.call-update
  7.9 0.0 reduce-scatter.2.cloned.1.call-start
  7.9 0.8 mul.118
  8.7 1.0 convert_element_type.22
  9.7 0.7 convert_multiply_fusion
  10.4 0.7 fusion.17
  11.0 0.8 add_divide_fusion.1
  11.8 0.1 broadcast_multiply_fusion.1
  11.9 53.5 %all-gather.2.cloned.1.call-done = bf16[512,4096]{1,0:T(8,128)(2,1)} async-done(((bf16[512,256]{1,0:T(8,128)(2,1)}), bf16[512,4096]{1,0:T(8,128)(2,1)}) %all-gather.2.cloned.1.call-update) | async-done | bytes 4194320 | tf_op jit(solution)/shard_map/all_gather | solution.py:45
  65.4 0.0 copy-start.1
  65.4 8.3 %subtract_convert_fusion = bf16[2,2,256,4096]{3,2,1,0:T(8,128)(2,1)S(1)} fusion(bf16[2,2,256,4096]{3,2,1,0:T(8,128)(2,1)} %param.6, bf16[512,4096]{1,0:T(8,128)(2,1)} %all-gather.2.cloned.1.call-done, f32[2,2,512]{2,1,0:T(2,128)S(1)} %get-tuple-element.7, f32[256,512]{1,0:T(8,128)S(1)} %convert_element_type.22), kind=kOutput, calls=%fused_computation | convolution fusion | flops 4308598784 | bytes 21504000 | tf_op jit(solution)/shard_map/dot_general | solution.py:47
  73.6 0.0 copy-start
  73.7 3.2 %copy-done = bf16[2,2,256,4096]{3,2,1,0:T(8,128)(2,1)} copy-done((bf16[2,2,256,4096]{3,2,1,0:T(8,128)(2,1)}, bf16[2,2,256,4096]{3,2,1,0:T(8,128)(2,1)S(1)}, u32[]{:S(2)}) %copy-start) | copy-done | bytes 8388632
  76.9 0.0 copy-done.1
  76.9 1.3 fusion.3
  78.2 2.9 %fusion.4 = f32[4096,512]{1,0:T(8,128)S(1)} fusion(bf16[256,512]{1,0:T(8,128)(2,1)S(1)} %copy-done.1, bf16[2,2,256,4096]{3,2,1,0:T(8,128)(2,1)} %copy-done), kind=kOutput, calls=%fused_computation.9 | convolution fusion | flops 1073741824 | bytes 10747904 | tf_op jit(solution)/shard_map/dot_general | solution.py:21
  81.1 6.1 %fusion.5 = f32[4096,512]{1,0:T(8,128)} fusion(bf16[256,512]{1,0:T(8,128)(2,1)S(1)} %copy-done.1, bf16[2,2,256,4096]{3,2,1,0:T(8,128)(2,1)} %copy-done), kind=kOutput, calls=%fused_computation.11 | convolution fusion | flops 1073741824 | bytes 10747904 | tf_op jit(solution)/shard_map/dot_general | solution.py:21
  87.2 8.4 %multiply_add_fusion = f32[4096,512]{1,0:T(8,128)} fusion(f32[4096,512]{1,0:T(8,128)S(1)} %fusion.3, f32[4096,512]{1,0:T(8,128)S(1)} %fusion.4, f32[4096,512]{1,0:T(8,128)} %fusion.5, bf16[256,512]{1,0:T(8,128)(2,1)S(1)} %copy-done.1, f32[512]{0:T(512)S(1)} %bitcast.60, f32[512]{0:T(512)S(1)} %bitcast.62, f32[512]{0:T(512)S(1)} %bitcast.64, ...), kind=kOutput, calls=%fused_computation.1 | convolution fusion | flops 1088421888 | bytes 35921920 | tf_op jit(solution)/shard_map/dot_general | solution.py:21
  95.6 0.0 reduce-scatter.2.cloned.1.call-update
  95.6 8.2 %fusion = f32[2,2,256,512]{3,2,1,0:T(8,128)S(1)} fusion(bf16[2,2,256,4096]{3,2,1,0:T(8,128)(2,1)} %copy-done, bf16[512,4096]{1,0:T(8,128)(2,1)} %all-gather.2.cloned.1.call-done), kind=kOutput, calls=%fused_computation.2 | convolution fusion | flops 4294967296 | bytes 14680064 | tf_op jit(solution)/shard_map/dot_general | solution.py:27
  103.9 1.0 fusion.10
  104.9 92.5 %reduce-scatter.2.cloned.1.call-done = f32[256,512]{1,0:T(8,128)} async-done(((f32[4096,512]{1,0:T(8,128)}), f32[256,512]{1,0:T(8,128)}) %reduce-scatter.2.cloned.1.call-update) | async-done | bytes 524304 | tf_op jit(solution)/shard_map/reduce_scatter | solution.py:65
  197.4 1.9 broadcast_multiply_fusion
  (1 shorter events, 0.0 us)
Async XLA Ops:
  7.2 58.2 %all-gather.2.cloned.1.call-start = ((), (), s32[]{:S(2)}) async-start(), calls=%async_computation.1 | async-start | bytes 4456448 | tf_op jit(solution)/shard_map/all_gather | solution.py:45
  7.9 189.5 %reduce-scatter.2.cloned.1.call-start = ((), (), s32[]{:S(2)}) async-start(), calls=%async_computation.2 | async-start | bytes 8912896 | tf_op jit(solution)/shard_map/reduce_scatter | solution.py:65
  65.4 11.5 %copy-start.1 = (bf16[256,512]{1,0:T(8,128)(2,1)S(1)}, bf16[256,512]{1,0:T(8,128)(2,1)}, u32[]{:S(2)}) copy-start(bf16[256,512]{1,0:T(8,128)(2,1)} %param.7) | copy-start | bytes 786436
  73.6 3.2 %copy-start = (bf16[2,2,256,4096]{3,2,1,0:T(8,128)(2,1)}, bf16[2,2,256,4096]{3,2,1,0:T(8,128)(2,1)S(1)}, u32[]{:S(2)}) copy-start(bf16[2,2,256,4096]{3,2,1,0:T(8,128)(2,1)S(1)} %subtract_convert_fusion) | copy-start | bytes 25165828
Sparse Core Ops, SparseCore 0:
  10.1 55.1 all-gather.1
  95.8 101.5 reduce-scatter.1
where the time goes:
time: 206 us
  waiting for transfers between devices  147 us (71%)
  matrix products  35.2 us (17%)
  between operations  14.1 us (7%)
  other arithmetic  6.84 us (3%)
  local copies, waits for them, and re-layouts  3.23 us (2%)
    reduce_scatter x1, waiting for transfers between devices, on_device(): lax.psum_scatter(running, 'port', scatter_dimension=0, tiled=True)  92.5 us
    all_gather x1, waiting for transfers between devices, on_device(): block_cols = lax.all_gather(in_factor, 'port', axis=1, tiled=True)  53.5 us
    dot_general x4, matrix products, contract_first(): lax.dot_general(left, right, (((0,), (0,)), ((), ())), preferred_element_...  18.7 us
    dot_general x1, matrix products, on_device(): jnp.dot(scaled.reshape(-1, pole_count), block_cols, preferred_element_typ...  8.27 us
    dot_general x1, matrix products, contract_second(): lax.dot_general(left, right, (((1,), (1,)), ((), ())), preferred_element_...  8.24 us
  transfers between devices with their start and end apart: 2, of which 2 were waited for; matrix products, arithmetic and copies ran while one was open for 6% of the time, Pallas kernels for 0%

commit v1 on v0

--- a/solution.py
+++ b/solution.py
@@ -42,7 +42,12 @@
     scaled = (
         out_factor.astype(jnp.float32)[None, None, :, :] * coefficients[:, :, None, :]
     ).astype(jnp.bfloat16)
-    block_cols = lax.all_gather(in_factor, "port", axis=1, tiled=True)
+    ring = [in_factor]
+    for hop in range(15):
+        ring.append(lax.ppermute(ring[-1], "port", [(dev, (dev + 1) % 16) for dev in range(16)]))
+    block_cols = jnp.roll(
+        jnp.concatenate(ring[::-1], axis=1), (lax.axis_index("port") + 1) * ring[0].shape[1], axis=1
+    )
     width_cols = block_cols.shape[1]
     model = jnp.dot(scaled.reshape(-1, pole_count), block_cols, preferred_element_type=jnp.float32)
     model = model.reshape(freq_count, 2, local_rows, width_cols)

time: 206 us -> 286 us (1.39)
  waiting for transfers between devices: 147 us -> 216 us
  local copies, waits for them, and re-layouts: 3.23 us -> 13.1 us
    ppermute x0 -> x15, waiting for transfers between devices: none -> 124 us  [on_device(): lax.ppermute(ring[-1], 'port', [(dev, (dev + 1) % 16) for dev in range(16)])]
    all_gather x1 -> x0, waiting for transfers between devices: 53.5 us -> none  [on_device(): block_cols = lax.all_gather(in_factor, 'port', axis=1, tiled=True)]
    unnamed x4 -> x41, local copies, waits for them, and re-layouts: 3.22 us -> 13 us
  transfers between devices with their start and end apart: 2 -> 16, of which waited for: 2 -> 16; matrix products, arithmetic and copies ran while one was open for 6% -> 5% of each run, Pallas kernels for 0% -> 0%
where the time goes in v1:
time: 286 us
  waiting for transfers between devices  216 us (76%)
  matrix products  34.3 us (12%)
  between operations  14.4 us (5%)
  local copies, waits for them, and re-layouts  13.1 us (5%)
  other arithmetic  7.63 us (3%)
    ppermute x15, waiting for transfers between devices, on_device(): lax.ppermute(ring[-1], 'port', [(dev, (dev + 1) % 16) for dev in range(16)])  124 us
    reduce_scatter x1, waiting for transfers between devices, on_device(): lax.psum_scatter(running, 'port', scatter_dimension=0, tiled=True)  91.8 us
    dot_general x4, matrix products, contract_first(): lax.dot_general(left, right, (((0,), (0,)), ((), ())), preferred_element_...  18.9 us
    unnamed x41, local copies, waits for them, and re-layouts  13 us
    dot_general x1, matrix products, contract_second(): lax.dot_general(left, right, (((1,), (1,)), ((), ())), preferred_element_...  8.42 us
    dot_general x1, matrix products, on_device(): jnp.dot(scaled.reshape(-1, pole_count), block_cols, preferred_element_typ...  7.06 us
  transfers between devices with their start and end apart: 16, of which 16 were waited for; matrix products, arithmetic and copies ran while one was open for 5% of the time, Pallas kernels for 0%

profile of v1, /device:TPU:0, one launch (start us, length us, event | category | flops | bytes accessed | tf_op | source)
XLA Modules:
  0.0 286.0 jit_solution(10098766306626322135)
XLA Ops:
  7.8 9.2 %collective-permute-done = bf16[512,256]{1,0:T(8,128)(2,1)S(1)} collective-permute-done((bf16[512,256]{1,0:T(8,128)(2,1)}, bf16[512,256]{1,0:T(8,128)(2,1)S(1)}, u32[]{:S(2)}, u32[]{:S(2)}) %collective-permute-start) | collective-permute-done | bytes 262176 | tf_op jit(solution)/shard_map/ppermute | solution.py:47
  17.0 8.5 %collective-permute-done.1 = bf16[512,256]{1,0:T(8,128)(2,1)S(1)} collective-permute-done((bf16[512,256]{1,0:T(8,128)(2,1)S(1)}, bf16[512,256]{1,0:T(8,128)(2,1)S(1)}, u32[]{:S(2)}, u32[]{:S(2)}) %collective-permute-start.1) | collective-permute-done | bytes 262176 | tf_op jit(solution)/shard_map/ppermute | solution.py:47
  25.5 8.5 %collective-permute-done.2 = bf16[512,256]{1,0:T(8,128)(2,1)S(1)} collective-permute-done((bf16[512,256]{1,0:T(8,128)(2,1)S(1)}, bf16[512,256]{1,0:T(8,128)(2,1)S(1)}, u32[]{:S(2)}, u32[]{:S(2)}) %collective-permute-start.2) | collective-permute-done | bytes 262176 | tf_op jit(solution)/shard_map/ppermute | solution.py:47
  34.0 8.5 %collective-permute-done.3 = bf16[512,256]{1,0:T(8,128)(2,1)S(1)} collective-permute-done((bf16[512,256]{1,0:T(8,128)(2,1)S(1)}, bf16[512,256]{1,0:T(8,128)(2,1)S(1)}, u32[]{:S(2)}, u32[]{:S(2)}) %collective-permute-start.3) | collective-permute-done | bytes 262176 | tf_op jit(solution)/shard_map/ppermute | solution.py:47
  42.5 8.5 %collective-permute-done.4 = bf16[512,256]{1,0:T(8,128)(2,1)S(1)} collective-permute-done((bf16[512,256]{1,0:T(8,128)(2,1)S(1)}, bf16[512,256]{1,0:T(8,128)(2,1)S(1)}, u32[]{:S(2)}, u32[]{:S(2)}) %collective-permute-start.4) | collective-permute-done | bytes 262176 | tf_op jit(solution)/shard_map/ppermute | solution.py:47
  51.0 8.5 %collective-permute-done.5 = bf16[512,256]{1,0:T(8,128)(2,1)S(1)} collective-permute-done((bf16[512,256]{1,0:T(8,128)(2,1)S(1)}, bf16[512,256]{1,0:T(8,128)(2,1)S(1)}, u32[]{:S(2)}, u32[]{:S(2)}) %collective-permute-start.5) | collective-permute-done | bytes 262176 | tf_op jit(solution)/shard_map/ppermute | solution.py:47
  59.5 8.5 %collective-permute-done.6 = bf16[512,256]{1,0:T(8,128)(2,1)S(1)} collective-permute-done((bf16[512,256]{1,0:T(8,128)(2,1)S(1)}, bf16[512,256]{1,0:T(8,128)(2,1)S(1)}, u32[]{:S(2)}, u32[]{:S(2)}) %collective-permute-start.6) | collective-permute-done | bytes 262176 | tf_op jit(solution)/shard_map/ppermute | solution.py:47
  68.0 8.5 %collective-permute-done.7 = bf16[512,256]{1,0:T(8,128)(2,1)S(1)} collective-permute-done((bf16[512,256]{1,0:T(8,128)(2,1)S(1)}, bf16[512,256]{1,0:T(8,128)(2,1)S(1)}, u32[]{:S(2)}, u32[]{:S(2)}) %collective-permute-start.7) | collective-permute-done | bytes 262176 | tf_op jit(solution)/shard_map/ppermute | solution.py:47
  76.5 8.5 %collective-permute-done.8 = bf16[512,256]{1,0:T(8,128)(2,1)S(1)} collective-permute-done((bf16[512,256]{1,0:T(8,128)(2,1)S(1)}, bf16[512,256]{1,0:T(8,128)(2,1)S(1)}, u32[]{:S(2)}, u32[]{:S(2)}) %collective-permute-start.8) | collective-permute-done | bytes 262176 | tf_op jit(solution)/shard_map/ppermute | solution.py:47
  85.0 8.5 %collective-permute-done.9 = bf16[512,256]{1,0:T(8,128)(2,1)S(1)} collective-permute-done((bf16[512,256]{1,0:T(8,128)(2,1)S(1)}, bf16[512,256]{1,0:T(8,128)(2,1)S(1)}, u32[]{:S(2)}, u32[]{:S(2)}) %collective-permute-start.9) | collective-permute-done | bytes 262176 | tf_op jit(solution)/shard_map/ppermute | solution.py:47
  93.5 8.5 %collective-permute-done.10 = bf16[512,256]{1,0:T(8,128)(2,1)S(1)} collective-permute-done((bf16[512,256]{1,0:T(8,128)(2,1)S(1)}, bf16[512,256]{1,0:T(8,128)(2,1)S(1)}, u32[]{:S(2)}, u32[]{:S(2)}) %collective-permute-start.10) | collective-permute-done | bytes 262176 | tf_op jit(solution)/shard_map/ppermute | solution.py:47
  102.0 8.5 %collective-permute-done.11 = bf16[512,256]{1,0:T(8,128)(2,1)S(1)} collective-permute-done((bf16[512,256]{1,0:T(8,128)(2,1)S(1)}, bf16[512,256]{1,0:T(8,128)(2,1)S(1)}, u32[]{:S(2)}, u32[]{:S(2)}) %collective-permute-start.11) | collective-permute-done | bytes 262176 | tf_op jit(solution)/shard_map/ppermute | solution.py:47
  111.1 7.9 %collective-permute-done.12 = bf16[512,256]{1,0:T(8,128)(2,1)} collective-permute-done((bf16[512,256]{1,0:T(8,128)(2,1)S(1)}, bf16[512,256]{1,0:T(8,128)(2,1)}, u32[]{:S(2)}, u32[]{:S(2)}) %collective-permute-start.12) | collective-permute-done | bytes 262176 | tf_op jit(solution)/shard_map/ppermute | solution.py:47
  121.2 6.6 %collective-permute-done.13 = bf16[512,256]{1,0:T(8,128)(2,1)} collective-permute-done((bf16[512,256]{1,0:T(8,128)(2,1)}, bf16[512,256]{1,0:T(8,128)(2,1)}, u32[]{:S(2)}, u32[]{:S(2)}) %collective-permute-start.13) | collective-permute-done | bytes 262176 | tf_op jit(solution)/shard_map/ppermute | solution.py:47
  127.9 1.8 convert_element_type.22
  129.8 6.9 %collective-permute-done.14 = bf16[512,256]{1,0:T(8,128)(2,1)} collective-permute-done((bf16[512,256]{1,0:T(8,128)(2,1)}, bf16[512,256]{1,0:T(8,128)(2,1)}, u32[]{:S(2)}, u32[]{:S(2)}) %collective-permute-start.14) | collective-permute-done | bytes 262176 | tf_op jit(solution)/shard_map/ppermute | solution.py:47
  137.7 1.0 constant_dynamic-update-slice_fusion.30
  138.6 1.0 constant_dynamic-update-slice_fusion.29
  140.1 1.0 constant_dynamic-update-slice_fusion.15
  141.1 1.0 constant_dynamic-update-slice_fusion.14
  142.1 1.0 constant_dynamic-update-slice_fusion.13
  143.5 3.2 %copy-done.4 = bf16[512,8192]{1,0:T(8,128)(2,1)} copy-done((bf16[512,8192]{1,0:T(8,128)(2,1)}, bf16[512,8192]{1,0:T(8,128)(2,1)S(1)}, u32[]{:S(2)}) %copy-start.4) | copy-done | bytes 8388632
  146.8 7.1 %subtract_convert_fusion = bf16[2,2,256,4096]{3,2,1,0:T(8,128)(2,1)S(1)} fusion(bf16[2,2,256,4096]{3,2,1,0:T(8,128)(2,1)} %param.6, bf16[512,8192]{1,0:T(8,128)(2,1)S(1)} %constant_dynamic-update-slice_fusion, s32[]{:T(128)S(6)} %select_n.14, f32[2,2,512]{2,1,0:T(2,128)S(1)} %get-tuple-element.7, f32[256,512]{1,0:T(8,128)S(1)} %copy-done.3), kind=kOutput, calls=%fused_computation | convolution fusion | flops 4308598784 | bytes 21504004 | tf_op jit(solution)/shard_map/dot_general | solution.py:52
  153.8 3.2 %copy-done = bf16[2,2,256,4096]{3,2,1,0:T(8,128)(2,1)} copy-done((bf16[2,2,256,4096]{3,2,1,0:T(8,128)(2,1)}, bf16[2,2,256,4096]{3,2,1,0:T(8,128)(2,1)S(1)}, u32[]{:S(2)}) %copy-start) | copy-done | bytes 8388632
  157.1 1.3 fusion.5
  158.4 2.9 %fusion.6 = f32[4096,512]{1,0:T(8,128)S(1)} fusion(bf16[256,512]{1,0:T(8,128)(2,1)S(1)} %copy-done.1, bf16[2,2,256,4096]{3,2,1,0:T(8,128)(2,1)} %copy-done), kind=kOutput, calls=%fused_computation.11 | convolution fusion | flops 1073741824 | bytes 10747904 | tf_op jit(solution)/shard_map/dot_general | solution.py:21
  161.3 6.1 %fusion.7 = f32[4096,512]{1,0:T(8,128)} fusion(bf16[256,512]{1,0:T(8,128)(2,1)S(1)} %copy-done.1, bf16[2,2,256,4096]{3,2,1,0:T(8,128)(2,1)} %copy-done), kind=kOutput, calls=%fused_computation.13 | convolution fusion | flops 1073741824 | bytes 10747904 | tf_op jit(solution)/shard_map/dot_general | solution.py:21
  167.4 8.5 %multiply_add_fusion = f32[4096,512]{1,0:T(8,128)} fusion(f32[4096,512]{1,0:T(8,128)S(1)} %fusion.5, f32[4096,512]{1,0:T(8,128)S(1)} %fusion.6, f32[4096,512]{1,0:T(8,128)} %fusion.7, bf16[256,512]{1,0:T(8,128)(2,1)S(1)} %copy-done.1, f32[512]{0:T(512)S(1)} %bitcast.60, f32[512]{0:T(512)S(1)} %bitcast.62, f32[512]{0:T(512)S(1)} %bitcast.64, ...), kind=kOutput, calls=%fused_computation.1 | convolution fusion | flops 1088421888 | bytes 35921920 | tf_op jit(solution)/shard_map/dot_general | solution.py:21
  176.0 8.4 %fusion = f32[2,2,256,512]{3,2,1,0:T(8,128)S(1)} fusion(bf16[2,2,256,4096]{3,2,1,0:T(8,128)(2,1)} %copy-done, bf16[512,8192]{1,0:T(8,128)(2,1)} %copy-done.4, s32[]{:T(128)S(6)} %select_n.14), kind=kOutput, calls=%fused_computation.2 | convolution fusion | flops 4294967296 | bytes 14680068 | tf_op jit(solution)/shard_map/dot_general | solution.py:27
  184.4 1.0 fusion.12
  185.4 91.8 %reduce-scatter.2.cloned.1.call-done = f32[256,512]{1,0:T(8,128)} async-done(((f32[4096,512]{1,0:T(8,128)}), f32[256,512]{1,0:T(8,128)}) %reduce-scatter.2.cloned.1.call-update) | async-done | bytes 524304 | tf_op jit(solution)/shard_map/reduce_scatter | solution.py:70
  277.2 1.9 broadcast_multiply_fusion
  (58 shorter events, 5.3 us)
Async XLA Ops:
  7.2 132.9 %copy-start.2 = (bf16[512,256]{1,0:T(8,128)(2,1)S(1)}, bf16[512,256]{1,0:T(8,128)(2,1)}, u32[]{:S(2)}) copy-start(bf16[512,256]{1,0:T(8,128)(2,1)} %param.8) | copy-start | bytes 786436
  7.2 270.1 %reduce-scatter.2.cloned.1.call-start = ((), (), s32[]{:S(2)}) async-start(), calls=%async_computation.1 | async-start | bytes 8912896 | tf_op jit(solution)/shard_map/reduce_scatter | solution.py:70
  7.2 9.8 %collective-permute-start = (bf16[512,256]{1,0:T(8,128)(2,1)}, bf16[512,256]{1,0:T(8,128)(2,1)S(1)}, u32[]{:S(2)}, u32[]{:S(2)}) collective-permute-start(bf16[512,256]{1,0:T(8,128)(2,1)} %param.8), channel_id=1, source_target_pairs={{0,1},{1,2},{2,3},{3,4},{4,5},{5,6},{6,7},{7,8},{8,9},{9,10},{10,1... | collective-permute-start | bytes 786440 | tf_op jit(solution)/shard_map/ppermute | solution.py:47
  17.0 8.5 %collective-permute-start.1 = (bf16[512,256]{1,0:T(8,128)(2,1)S(1)}, bf16[512,256]{1,0:T(8,128)(2,1)S(1)}, u32[]{:S(2)}, u32[]{:S(2)}) collective-permute-start(bf16[512,256]{1,0:T(8,128)(2,1)S(1)} %collective-permute-done), channel_id=1, source_target_pairs={{0,1},{1,2},{2,3},{3,4},{4,5},{5,6},{6,7},{7,8},{8,9},{9,10},{10,1... | collective-permute-start | bytes 786440 | tf_op jit(solution)/shard_map/ppermute | solution.py:47
  25.5 8.5 %collective-permute-start.2 = (bf16[512,256]{1,0:T(8,128)(2,1)S(1)}, bf16[512,256]{1,0:T(8,128)(2,1)S(1)}, u32[]{:S(2)}, u32[]{:S(2)}) collective-permute-start(bf16[512,256]{1,0:T(8,128)(2,1)S(1)} %collective-permute-done.1), channel_id=1, source_target_pairs={{0,1},{1,2},{2,3},{3,4},{4,5},{5,6},{6,7},{7,8},{8,9},{9,10},{10,1... | collective-permute-start | bytes 786440 | tf_op jit(solution)/shard_map/ppermute | solution.py:47
  34.0 8.5 %collective-permute-start.3 = (bf16[512,256]{1,0:T(8,128)(2,1)S(1)}, bf16[512,256]{1,0:T(8,128)(2,1)S(1)}, u32[]{:S(2)}, u32[]{:S(2)}) collective-permute-start(bf16[512,256]{1,0:T(8,128)(2,1)S(1)} %collective-permute-done.2), channel_id=1, source_target_pairs={{0,1},{1,2},{2,3},{3,4},{4,5},{5,6},{6,7},{7,8},{8,9},{9,10},{10,1... | collective-permute-start | bytes 786440 | tf_op jit(solution)/shard_map/ppermute | solution.py:47
  42.5 8.5 %collective-permute-start.4 = (bf16[512,256]{1,0:T(8,128)(2,1)S(1)}, bf16[512,256]{1,0:T(8,128)(2,1)S(1)}, u32[]{:S(2)}, u32[]{:S(2)}) collective-permute-start(bf16[512,256]{1,0:T(8,128)(2,1)S(1)} %collective-permute-done.3), channel_id=1, source_target_pairs={{0,1},{1,2},{2,3},{3,4},{4,5},{5,6},{6,7},{7,8},{8,9},{9,10},{10,1... | collective-permute-start | bytes 786440 | tf_op jit(solution)/shard_map/ppermute | solution.py:47
  51.0 8.5 %collective-permute-start.5 = (bf16[512,256]{1,0:T(8,128)(2,1)S(1)}, bf16[512,256]{1,0:T(8,128)(2,1)S(1)}, u32[]{:S(2)}, u32[]{:S(2)}) collective-permute-start(bf16[512,256]{1,0:T(8,128)(2,1)S(1)} %collective-permute-done.4), channel_id=1, source_target_pairs={{0,1},{1,2},{2,3},{3,4},{4,5},{5,6},{6,7},{7,8},{8,9},{9,10},{10,1... | collective-permute-start | bytes 786440 | tf_op jit(solution)/shard_map/ppermute | solution.py:47
  59.5 8.5 %collective-permute-start.6 = (bf16[512,256]{1,0:T(8,128)(2,1)S(1)}, bf16[512,256]{1,0:T(8,128)(2,1)S(1)}, u32[]{:S(2)}, u32[]{:S(2)}) collective-permute-start(bf16[512,256]{1,0:T(8,128)(2,1)S(1)} %collective-permute-done.5), channel_id=1, source_target_pairs={{0,1},{1,2},{2,3},{3,4},{4,5},{5,6},{6,7},{7,8},{8,9},{9,10},{10,1... | collective-permute-start | bytes 786440 | tf_op jit(solution)/shard_map/ppermute | solution.py:47
  68.0 8.5 %collective-permute-start.7 = (bf16[512,256]{1,0:T(8,128)(2,1)S(1)}, bf16[512,256]{1,0:T(8,128)(2,1)S(1)}, u32[]{:S(2)}, u32[]{:S(2)}) collective-permute-start(bf16[512,256]{1,0:T(8,128)(2,1)S(1)} %collective-permute-done.6), channel_id=1, source_target_pairs={{0,1},{1,2},{2,3},{3,4},{4,5},{5,6},{6,7},{7,8},{8,9},{9,10},{10,1... | collective-permute-start | bytes 786440 | tf_op jit(solution)/shard_map/ppermute | solution.py:47
  76.5 8.5 %collective-permute-start.8 = (bf16[512,256]{1,0:T(8,128)(2,1)S(1)}, bf16[512,256]{1,0:T(8,128)(2,1)S(1)}, u32[]{:S(2)}, u32[]{:S(2)}) collective-permute-start(bf16[512,256]{1,0:T(8,128)(2,1)S(1)} %collective-permute-done.7), channel_id=1, source_target_pairs={{0,1},{1,2},{2,3},{3,4},{4,5},{5,6},{6,7},{7,8},{8,9},{9,10},{10,1... | collective-permute-start | bytes 786440 | tf_op jit(solution)/shard_map/ppermute | solution.py:47
  85.0 8.5 %collective-permute-start.9 = (bf16[512,256]{1,0:T(8,128)(2,1)S(1)}, bf16[512,256]{1,0:T(8,128)(2,1)S(1)}, u32[]{:S(2)}, u32[]{:S(2)}) collective-permute-start(bf16[512,256]{1,0:T(8,128)(2,1)S(1)} %collective-permute-done.8), channel_id=1, source_target_pairs={{0,1},{1,2},{2,3},{3,4},{4,5},{5,6},{6,7},{7,8},{8,9},{9,10},{10,1... | collective-permute-start | bytes 786440 | tf_op jit(solution)/shard_map/ppermute | solution.py:47
  93.5 8.5 %collective-permute-start.10 = (bf16[512,256]{1,0:T(8,128)(2,1)S(1)}, bf16[512,256]{1,0:T(8,128)(2,1)S(1)}, u32[]{:S(2)}, u32[]{:S(2)}) collective-permute-start(bf16[512,256]{1,0:T(8,128)(2,1)S(1)} %collective-permute-done.9), channel_id=1, source_target_pairs={{0,1},{1,2},{2,3},{3,4},{4,5},{5,6},{6,7},{7,8},{8,9},{9,10},{10,1... | collective-permute-start | bytes 786440 | tf_op jit(solution)/shard_map/ppermute | solution.py:47
  102.0 8.5 %collective-permute-start.11 = (bf16[512,256]{1,0:T(8,128)(2,1)S(1)}, bf16[512,256]{1,0:T(8,128)(2,1)S(1)}, u32[]{:S(2)}, u32[]{:S(2)}) collective-permute-start(bf16[512,256]{1,0:T(8,128)(2,1)S(1)} %collective-permute-done.10), channel_id=1, source_target_pairs={{0,1},{1,2},{2,3},{3,4},{4,5},{5,6},{6,7},{7,8},{8,9},{9,10},{10,1... | collective-permute-start | bytes 786440 | tf_op jit(solution)/shard_map/ppermute | solution.py:47
  110.5 8.6 %collective-permute-start.12 = (bf16[512,256]{1,0:T(8,128)(2,1)S(1)}, bf16[512,256]{1,0:T(8,128)(2,1)}, u32[]{:S(2)}, u32[]{:S(2)}) collective-permute-start(bf16[512,256]{1,0:T(8,128)(2,1)S(1)} %collective-permute-done.11), channel_id=1, source_target_pairs={{0,1},{1,2},{2,3},{3,4},{4,5},{5,6},{6,7},{7,8},{8,9},{9,10},{10,1... | collective-permute-start | bytes 786440 | tf_op jit(solution)/shard_map/ppermute | solution.py:47
  119.1 8.8 %collective-permute-start.13 = (bf16[512,256]{1,0:T(8,128)(2,1)}, bf16[512,256]{1,0:T(8,128)(2,1)}, u32[]{:S(2)}, u32[]{:S(2)}) collective-permute-start(bf16[512,256]{1,0:T(8,128)(2,1)} %collective-permute-done.12), channel_id=1, source_target_pairs={{0,1},{1,2},{2,3},{3,4},{4,5},{5,6},{6,7},{7,8},{8,9},{9,10},{10,1... | collective-permute-start | bytes 786440 | tf_op jit(solution)/shard_map/ppermute | solution.py:47
  127.9 8.8 %collective-permute-start.14 = (bf16[512,256]{1,0:T(8,128)(2,1)}, bf16[512,256]{1,0:T(8,128)(2,1)}, u32[]{:S(2)}, u32[]{:S(2)}) collective-permute-start(bf16[512,256]{1,0:T(8,128)(2,1)} %collective-permute-done.13), channel_id=1, source_target_pairs={{0,1},{1,2},{2,3},{3,4},{4,5},{5,6},{6,7},{7,8},{8,9},{9,10},{10,1... | collective-permute-start | bytes 786440 | tf_op jit(solution)/shard_map/ppermute | solution.py:47
  129.8 17.0 %copy-start.3 = (f32[256,512]{1,0:T(8,128)S(1)}, f32[256,512]{1,0:T(8,128)}, u32[]{:S(2)}) copy-start(f32[256,512]{1,0:T(8,128)} %convert_element_type.22) | copy-start | bytes 1572868
  143.5 3.2 %copy-start.4 = (bf16[512,8192]{1,0:T(8,128)(2,1)}, bf16[512,8192]{1,0:T(8,128)(2,1)S(1)}, u32[]{:S(2)}) copy-start(bf16[512,8192]{1,0:T(8,128)(2,1)S(1)} %constant_dynamic-update-slice_fusion) | copy-start | bytes 25165828
  146.8 10.3 %copy-start.1 = (bf16[256,512]{1,0:T(8,128)(2,1)S(1)}, bf16[256,512]{1,0:T(8,128)(2,1)}, u32[]{:S(2)}) copy-start(bf16[256,512]{1,0:T(8,128)(2,1)} %param.7) | copy-start | bytes 786436
  153.8 3.2 %copy-start = (bf16[2,2,256,4096]{3,2,1,0:T(8,128)(2,1)}, bf16[2,2,256,4096]{3,2,1,0:T(8,128)(2,1)S(1)}, u32[]{:S(2)}) copy-start(bf16[2,2,256,4096]{3,2,1,0:T(8,128)(2,1)S(1)} %subtract_convert_fusion) | copy-start | bytes 25165828
Sparse Core Ops, SparseCore 0:
  176.1 101.1 reduce-scatter.1
